TPU v7x, 32 devices: a whole 2x2x4 slice. The times are simulated.
32 devices in a mesh: row: 8 (over y, x, core), col: 4 (over z).
Axes of the slice: x: 2, y: 2, z: 4, core: 2. Of those that a mesh axis runs over, the one named last changes fastest.
Arguments:
- fast_pos: float32 [3, 4096], P(None, ('row', 'col')), may hold values from 0 to 1
- fast_vel: float32 [3, 4096], P(None, ('row', 'col')), may hold values from -5 to 5
- fast_charge: float32 [4096], replicated, may hold values from -4 to 4
- fast_owner: int32 [4096], replicated, may hold values from 0 to 1023, as said below
- exclusions: int32 [4096, 4], replicated, may hold values from 0 to 4095, as said below
- slow_pos: float32 [3, 32, 32, 128], P(None, 'row', 'col'), may hold values from 0 to 1
- slow_vel: float32 [3, 32, 32, 128], P(None, 'row', 'col'), may hold values from -5 to 5
- slow_charge: float32 [32, 32, 128], P('row', 'col'), may hold values from -4 to 4
- neighbours: int32 [32, 32, 5], P('row', 'col'), may hold values from 0 to 24, all different within a row
Outputs:
- fast_pos_out: float32 [3, 4096], P(None, ('row', 'col'))
- fast_vel_out: float32 [3, 4096], P(None, ('row', 'col'))
- slow_pos_out: float32 [3, 32, 32, 128], P(None, 'row', 'col')
- slow_vel_out: float32 [3, 32, 32, 128], P(None, 'row', 'col')
Inputs may be any that keep to these rules, and one draw needn't show every extreme that they name: `fast_owner`: atoms a and b with a % (256) == b % (256) share an owner. `exclusions`: the partners of atom a are atoms b != a with b % (256) == a % 256; a partner may repeat. `neighbours`: the entries of one cell are distinct.
All inputs are finite; a program needn't handle non-finite values.
Results may differ from a plain program's by a relative error of at most 0.0003.
Values sent between devices are 32-bit elements; how exact they have to be, the bound alone decides.
No kernel may reach another device: no remote copies, remote signals or barrier semaphores. Data moves between devices by JAX's collectives and lax.ppermute only.
A program may use at most 64 MiB of HBM per device.

v0:
```python
import jax
import jax.numpy as jnp
from jax import lax
from jax.sharding import PartitionSpec as P

FAST = 4096
CELL = 128
INNER = 4
fast_coupling = 1.0
slow_coupling = 0.1
outer_dt = 0.2


def with_halo(x, sides, width):
    for axis, dim in sides:
        count, length = (lax.axis_size(axis), x.shape[dim])
        up = [(i, (i + 1) % count) for i in range(count)]
        down = [(j, i) for i, j in up]
        last = lax.slice_in_dim(x, length - width, length, axis=dim)
        initial = lax.slice_in_dim(x, 0, width, axis=dim)
        before = lax.ppermute(last, axis, up)
        after = lax.ppermute(initial, axis, down)
        x = jnp.concatenate([before, x, after], axis=dim)
    return x


def owner_coords(owner, total_cols):
    grid_row = (owner // total_cols).astype(jnp.float32)
    grid_col = (owner % total_cols).astype(jnp.float32)
    return jnp.stack([grid_row, grid_col, jnp.zeros_like(grid_row)])


def pair_fast(pos_a, cell_a, charge_a, exclude_a, pos_b, cell_b, charge_b, index_b):
    delta = pos_a[:, :, None] - pos_b[:, None, :] + (cell_a[:, :, None] - cell_b[:, None, :])
    dist_sq = jnp.sum(delta * delta, axis=0) + 1.0
    inverse = 1.0 / (dist_sq * jnp.sqrt(dist_sq))
    barred = jnp.any(exclude_a[:, :, None] == index_b[None, None, :], axis=1)
    weight = jnp.where(barred, jnp.float32(0.0), charge_a[:, None] * charge_b[None, :] * inverse)
    return fast_coupling * jnp.sum(weight[None] * delta, axis=2)


def slow_cells(own, views, lists):
    force = jnp.zeros((3,) + own.shape[1:], jnp.float32)
    offsets = jnp.arange(25, dtype=jnp.int32)
    for slot in range(lists.shape[-1]):
        chosen = lists[..., slot]
        pick = (chosen[..., None] == offsets).astype(jnp.float32)
        other = jnp.einsum("abo,oxabn->xabn", pick, views, precision=lax.Precision.HIGHEST)
        shift_row = (chosen // 5 - 2).astype(jnp.float32)
        shift_col = (chosen % 5 - 2).astype(jnp.float32)
        shift = jnp.stack([shift_row, shift_col, jnp.zeros_like(shift_row)])
        delta = own[0:3, :, :, :, None] - (other[0:3, :, :, None, :] + shift[:, :, :, None, None])
        dist_sq = jnp.sum(delta * delta, axis=0) + 0.5
        inverse = 1.0 / (dist_sq * jnp.sqrt(dist_sq))
        weight = other[3][:, :, None, :] * inverse
        force = force + jnp.sum(weight[None] * delta, axis=-1)
    return slow_coupling * own[3][None] * force


def fast_from_cells(frac, charge, picked):
    delta = frac[:, :, None] - picked[0:3]
    dist_sq = jnp.sum(delta * delta, axis=0) + 0.5
    inverse = 1.0 / (dist_sq * jnp.sqrt(dist_sq))
    weight = picked[3] * inverse
    return slow_coupling * charge[None, :] * jnp.sum(weight[None] * delta, axis=-1)


def per_device(
    fast_pos,
    fast_vel,
    fast_charge,
    fast_owner,
    exclusions,
    slow_pos,
    slow_vel,
    slow_charge,
    neighbours,
):
    row_count = lax.axis_size("row")
    col_count = lax.axis_size("col")
    row_index = lax.axis_index("row")
    col_index = lax.axis_index("col")
    flat_index = row_index * col_count + col_index
    piece = fast_pos.shape[1]
    cell_rows = slow_pos.shape[1]
    cell_cols = slow_pos.shape[2]
    total_cols = cell_cols * col_count
    coords = owner_coords(fast_owner, total_cols)
    block_width = col_count * piece
    block_start = row_index * block_width
    rows_cells = lax.dynamic_slice_in_dim(coords, block_start, block_width, 1)
    rows_charge = lax.dynamic_slice_in_dim(fast_charge, block_start, block_width, 0)
    rows_exclude = lax.dynamic_slice_in_dim(exclusions, block_start, block_width, 0)
    column_atoms = (
        (jnp.arange(row_count, dtype=jnp.int32) * col_count + col_index)[:, None] * piece
        + jnp.arange(piece, dtype=jnp.int32)[None, :]
    ).reshape(-1)
    column_cells = jnp.take(coords, column_atoms, axis=1)
    column_charge = jnp.take(fast_charge, column_atoms, axis=0)

    def fast_force(frac):
        rows_pos = lax.all_gather(frac, "col", axis=1, tiled=True)
        cols_pos = lax.all_gather(frac, "row", axis=1, tiled=True)
        partial_force = pair_fast(
            rows_pos,
            rows_cells,
            rows_charge,
            rows_exclude,
            cols_pos,
            column_cells,
            column_charge,
            column_atoms,
        )
        return lax.psum_scatter(partial_force, "col", scatter_dimension=1, tiled=True)

    grid_row = fast_owner // total_cols - row_index * cell_rows
    grid_col = fast_owner % total_cols - col_index * cell_cols
    inside = (grid_row >= 0) & (grid_row < cell_rows) & (grid_col >= 0) & (grid_col < cell_cols)
    local_cell = grid_row * cell_cols + grid_col
    cell_ids = jnp.arange(cell_rows * cell_cols, dtype=jnp.int32)
    select = jnp.where(
        inside[:, None] & (local_cell[:, None] == cell_ids[None, :]),
        jnp.float32(1.0),
        jnp.float32(0.0),
    )

    def slow_both(spos, frac):
        data = jnp.concatenate([spos, slow_charge[None]], axis=0)
        padded = with_halo(data, (("row", 1), ("col", 2)), 2)
        views = jnp.stack(
            [padded[:, o // 5 : o // 5 + cell_rows, o % 5 : o % 5 + cell_cols] for o in range(25)]
        )
        cell_force = slow_cells(data, views, neighbours)
        everyone = lax.all_gather(frac, ("row", "col"), axis=1, tiled=True)
        table = jnp.transpose(data, (1, 2, 0, 3)).reshape(cell_rows * cell_cols, 4 * CELL)
        picked = jnp.dot(
            select, table, precision=lax.Precision.HIGHEST, preferred_element_type=jnp.float32
        )
        picked = jnp.transpose(picked.reshape(FAST, 4, CELL), (1, 0, 2))
        partial_env = fast_from_cells(everyone, fast_charge, picked)
        summed = lax.psum(partial_env, ("row", "col"))
        own_env = lax.dynamic_slice_in_dim(summed, flat_index * piece, piece, 1)
        return (cell_force, own_env)

    half_outer = 0.5 * outer_dt
    inner_dt = outer_dt / INNER
    fast_acc = fast_force(fast_pos)
    slow_acc, env_acc = slow_both(slow_pos, fast_pos)
    slow_vel = slow_vel + half_outer * slow_acc
    fast_vel = fast_vel + half_outer * env_acc
    for inner_step in range(INNER):
        fast_vel = fast_vel + 0.5 * inner_dt * fast_acc
        fast_pos = fast_pos + inner_dt * fast_vel
        fast_acc = fast_force(fast_pos)
        fast_vel = fast_vel + 0.5 * inner_dt * fast_acc
    slow_pos = slow_pos + outer_dt * slow_vel
    slow_acc, env_acc = slow_both(slow_pos, fast_pos)
    slow_vel = slow_vel + half_outer * slow_acc
    fast_vel = fast_vel + half_outer * env_acc
    return (fast_pos, fast_vel, slow_pos, slow_vel)


def solution(mesh):
    return jax.shard_map(
        per_device,
        mesh=mesh,
        in_specs=(
            P(None, ("row", "col")),
            P(None, ("row", "col")),
            P(),
            P(),
            P(),
            P(None, "row", "col", None),
            P(None, "row", "col", None),
            P("row", "col", None),
            P("row", "col", None),
        ),
        out_specs=(
            P(None, ("row", "col")),
            P(None, ("row", "col")),
            P(None, "row", "col", None),
            P(None, "row", "col", None),
        ),
        check_vma=False,
    )
```

profile of v0, /device:TPU:0, one launch (start us, length us, event | category | flops | bytes accessed | tf_op | source)
XLA Modules:
  0.0 525.7 jit_solution(1581385438300912036)
XLA Ops:
  8.5 2.9 collective-permute-start.1
  11.6 9.6 %all_gather.38 = f32[3,1024]{1,0:T(4,128)S(1)} all-gather(f32[3,128]{1,0:T(4,128)} %param.9), channel_id=1, replica_groups=mesh['row'=8,'col'=4] {'row'}, dimensions={1}, use_global_device_ids=true | all-gather | bytes 13824 | tf_op jit(solution)/shard_map/all_gather | solution.py:103
  21.2 12.3 %all_gather.37 = f32[3,512]{1,0:T(4,128)S(1)} all-gather(f32[3,128]{1,0:T(4,128)} %param.9), channel_id=1, replica_groups=mesh['row'=8,'col'=4] {'col'}, dimensions={1}, use_global_device_ids=true | all-gather | bytes 7680 | tf_op jit(solution)/shard_map/all_gather | solution.py:102
  35.2 6.1 %gather_fusion = f32[1024]{0:T(1024)S(1)} fusion(f32[4096]{0:T(1024)S(1)} %copy-done.2, s32[1024]{0:T(1024)S(1)} %broadcast_clamp_fusion), kind=kCustom, calls=%fused_computation | custom fusion | bytes 12288 | tf_op jit(solution)/shard_map/jit(_take)/gather | solution.py:99
  41.3 2.8 gather_fusion.1
  51.6 65.5 %all_gather.36 = f32[3,4096]{1,0:T(4,128)S(1)} all-gather(f32[3,128]{1,0:T(4,128)S(1)} %copy-done.7), channel_id=1, replica_groups=mesh['row'=8,'col'=4] {'row','col'}, dimensions={1}, use_global_device_ids=true | all-gather | bytes 50688 | tf_op jit(solution)/shard_map/all_gather | solution.py:134
  117.2 6.8 %convolution_bitcast_fusion.1 = f32[4,4096,128]{1,2,0:T(8,128)S(1)} fusion(s32[4096]{0:T(1024)S(1)} %get-tuple-element.54, pred[4096]{0:T(1024)(128)(4,1)S(1)} %compare_and_fusion, f32[1,4,8,128]{3,2,0,1:T(8,128)S(1)} %bitcast.458, f32[3,4,8,128]{3,2,1,0:T(8,128)S(1)} %copy-done.3), kind=kOutput, calls=%fused_computation.29 | convolution fusion | flops 805715968 | bytes 8474624 | tf_op jit(solution)/shard_map/dot_general | solution.py:136
  126.9 38.7 %psum.14 = f32[3,4096]{1,0:T(4,128)S(1)} all-reduce(f32[3,4096]{1,0:T(4,128)S(1)} %broadcast_multiply_fusion.1), channel_id=1, replica_groups=mesh['row'=8,'col'=4] {'row','col'}, use_global_device_ids=true, to_apply=%region_2.3 | all-reduce | flops 12288 | bytes 98304 | tf_op jit(solution)/shard_map/psum | solution.py:141
  166.5 9.7 %all_gather.40 = f32[3,1024]{1,0:T(4,128)S(1)} all-gather(f32[3,128]{1,0:T(4,128)S(1)} %get-tuple-element.36), channel_id=1, replica_groups=mesh['row'=8,'col'=4] {'row'}, dimensions={1}, use_global_device_ids=true | all-gather | bytes 13824 | tf_op jit(solution)/shard_map/all_gather | solution.py:103
  176.2 12.1 %all_gather.39 = f32[3,512]{1,0:T(4,128)S(1)} all-gather(f32[3,128]{1,0:T(4,128)S(1)} %get-tuple-element.36), channel_id=1, replica_groups=mesh['row'=8,'col'=4] {'col'}, dimensions={1}, use_global_device_ids=true | all-gather | bytes 7680 | tf_op jit(solution)/shard_map/all_gather | solution.py:102
  193.7 17.6 %reduce-scatter.18.cloned.1.call-done = f32[128,3]{1,0:T(8,128)} async-done(((f32[512,3]{1,0:T(8,128)}), f32[128,3]{1,0:T(8,128)}) %reduce-scatter.18.cloned.1.call-update) | async-done | bytes 1552
  212.3 8.9 %all_gather.42 = f32[3,1024]{1,0:T(4,128)S(1)} all-gather(f32[3,128]{1,0:T(4,128)S(1)} %multiply_add_fusion.7), channel_id=1, replica_groups=mesh['row'=8,'col'=4] {'row'}, dimensions={1}, use_global_device_ids=true | all-gather | bytes 13824 | tf_op jit(solution)/shard_map/all_gather | solution.py:103
  221.2 11.9 %all_gather.41 = f32[3,512]{1,0:T(4,128)S(1)} all-gather(f32[3,128]{1,0:T(4,128)S(1)} %multiply_add_fusion.7), channel_id=1, replica_groups=mesh['row'=8,'col'=4] {'col'}, dimensions={1}, use_global_device_ids=true | all-gather | bytes 7680 | tf_op jit(solution)/shard_map/all_gather | solution.py:102
  238.5 3.8 collective-permute-start.3
  242.4 13.8 %reduce-scatter.20.cloned.1.call-done = f32[128,3]{1,0:T(8,128)} async-done(((f32[512,3]{1,0:T(8,128)}), f32[128,3]{1,0:T(8,128)}) %reduce-scatter.20.cloned.1.call-update) | async-done | bytes 1552
  257.1 8.9 %all_gather.44 = f32[3,1024]{1,0:T(4,128)S(1)} all-gather(f32[3,128]{1,0:T(4,128)S(1)} %get-tuple-element.34), channel_id=1, replica_groups=mesh['row'=8,'col'=4] {'row'}, dimensions={1}, use_global_device_ids=true | all-gather | bytes 13824 | tf_op jit(solution)/shard_map/all_gather | solution.py:103
  266.0 11.9 %all_gather.43 = f32[3,512]{1,0:T(4,128)S(1)} all-gather(f32[3,128]{1,0:T(4,128)S(1)} %get-tuple-element.34), channel_id=1, replica_groups=mesh['row'=8,'col'=4] {'col'}, dimensions={1}, use_global_device_ids=true | all-gather | bytes 7680 | tf_op jit(solution)/shard_map/all_gather | solution.py:102
  283.2 17.7 %reduce-scatter.22.cloned.1.call-done = f32[128,3]{1,0:T(8,128)} async-done(((f32[512,3]{1,0:T(8,128)}), f32[128,3]{1,0:T(8,128)}) %reduce-scatter.22.cloned.1.call-update) | async-done | bytes 1552
  301.8 8.9 %all_gather.46 = f32[3,1024]{1,0:T(4,128)S(1)} all-gather(f32[3,128]{1,0:T(4,128)S(1)} %multiply_add_fusion.5), channel_id=1, replica_groups=mesh['row'=8,'col'=4] {'row'}, dimensions={1}, use_global_device_ids=true | all-gather | bytes 13824 | tf_op jit(solution)/shard_map/all_gather | solution.py:103
  310.7 12.3 %all_gather.45 = f32[3,512]{1,0:T(4,128)S(1)} all-gather(f32[3,128]{1,0:T(4,128)S(1)} %multiply_add_fusion.5), channel_id=1, replica_groups=mesh['row'=8,'col'=4] {'col'}, dimensions={1}, use_global_device_ids=true | all-gather | bytes 7680 | tf_op jit(solution)/shard_map/all_gather | solution.py:102
  328.3 63.9 %all_gather.47 = f32[3,4096]{1,0:T(4,128)S(1)} all-gather(f32[3,128]{1,0:T(4,128)S(1)} %multiply_add_fusion.5), channel_id=1, replica_groups=mesh['row'=8,'col'=4] {'row','col'}, dimensions={1}, use_global_device_ids=true | all-gather | bytes 50688 | tf_op jit(solution)/shard_map/all_gather | solution.py:134
  403.4 2.5 fusion.2
  407.5 7.2 %fusion.3 = (f32[3,4,8,128]{3,2,1,0:T(8,128)S(1)}, f32[4,8,128,128]{3,2,1,0:T(8,128)S(1)}, f32[4,8,128,128]{3,2,1,0:T(8,128)S(1)}, f32[4,8,128,128]{3,2,1,0:T(8,128)S(1)}, f32[3,4,8,128]{3,2,1,0:T(8,128)S(1)}) fusion(f32[4,8,128,128]{3,2,1,0:T(8,128)S(1)} %fusion.51, f32[3,4,8,128]{3,2,1,0:T(8,128)S(1)} %slice_add_fusion.8, ...), kind=kLoop, calls=%fused_computation.33 | loop fusion | flops 21995520 | bytes 10878976 | tf_op jit(solution)/shard_map/reduce_sum | solution.py:56
  417.0 8.3 %fusion.5 = (f32[3,4,8,128]{3,2,1,0:T(8,128)S(1)}, f32[3,4,8,128]{3,2,1,0:T(8,128)S(1)}, f32[3,4,8,128]{3,2,1,0:T(8,128)S(1)}) fusion(f32[4,8,128,128]{3,2,1,0:T(8,128)S(1)} %fusion.53, f32[3,4,8,128]{3,2,1,0:T(8,128)S(1)} %slice_add_fusion.7, f32[3,4,8,128]{3,2,1,0:T(8,128)S(1)} %copy-done.3, f32[3,4,8,128]{3,2,1,0:T(8,128)S(1)} %slice_add_fusion.5, ...), kind=kLoop, calls=%fused_computation.35 | loop fusion | flops 14118912 | bytes 6635520 | tf_op jit(solution)/shard_map/reduce_sum | solution.py:56
  425.4 6.8 %convolution_bitcast_fusion = f32[4,4096,128]{1,2,0:T(8,128)S(1)} fusion(s32[4096]{0:T(1024)S(1)} %get-tuple-element.54, pred[4096]{0:T(1024)(128)(4,1)S(1)} %compare_and_fusion, f32[1,4,8,128]{3,2,1,0:T(8,128)S(1)} %bitcast.464, f32[3,4,8,128]{3,2,1,0:T(8,128)S(1)} %get-tuple-element.32), kind=kOutput, calls=%fused_computation.28 | convolution fusion | flops 805715968 | bytes 8474624 | tf_op jit(solution)/shard_map/dot_general | solution.py:136
  432.2 2.6 collective-permute-start.5
  437.6 40.2 %psum.15 = f32[3,4096]{1,0:T(4,128)S(1)} all-reduce(f32[3,4096]{1,0:T(4,128)S(1)} %broadcast_multiply_fusion), channel_id=1, replica_groups=mesh['row'=8,'col'=4] {'row','col'}, use_global_device_ids=true, to_apply=%region_31.32 | all-reduce | flops 12288 | bytes 98304 | tf_op jit(solution)/shard_map/psum | solution.py:141
  478.4 4.2 collective-permute-start.7
  484.7 2.3 fusion.28
  496.6 2.5 fusion.12
  500.7 7.2 %fusion.13 = (f32[3,4,8,128]{3,2,1,0:T(8,128)S(1)}, f32[4,8,128,128]{3,2,1,0:T(8,128)S(1)}, f32[4,8,128,128]{3,2,1,0:T(8,128)S(1)}, f32[4,8,128,128]{3,2,1,0:T(8,128)S(1)}, f32[3,4,8,128]{3,2,1,0:T(8,128)S(1)}) fusion(f32[4,8,128,128]{3,2,1,0:T(8,128)S(1)} %fusion.64, f32[3,4,8,128]{3,2,1,0:T(8,128)S(1)} %slice_add_fusion.3, ...), kind=kLoop, calls=%fused_computation.43 | loop fusion | flops 21995520 | bytes 10878976 | tf_op jit(solution)/shard_map/reduce_sum | solution.py:56
  510.2 8.1 %fusion.15 = (f32[3,4,8,128]{3,2,1,0:T(8,128)S(1)}, f32[3,4,8,128]{3,2,1,0:T(8,128)S(1)}, f32[3,4,8,128]{3,2,1,0:T(8,128)S(1)}) fusion(f32[4,8,128,128]{3,2,1,0:T(8,128)S(1)} %fusion.66, f32[3,4,8,128]{3,2,1,0:T(8,128)S(1)} %slice_add_fusion.2, f32[3,4,8,128]{3,2,1,0:T(8,128)S(1)} %get-tuple-element.32, f32[3,4,8,128]{3,2,1,0:T(8,128)S(1)} %slice_add_fusion, ...), kind=kLoop, calls=%fused_computation.45 | loop fusion | flops 14118912 | bytes 6635520 | tf_op jit(solution)/shard_map/reduce_sum | solution.py:56
  (220 shorter events, 72.3 us)
Async XLA Ops:
  7.2 37.4 %copy-start = (s32[4096,4]{0,1:T(4,128)S(1)}, s32[4096,4]{0,1:T(4,128)}, u32[]{:S(2)}) copy-start(s32[4096,4]{0,1:T(4,128)} %param.13) | copy-start | bytes 196612
  7.2 27.9 %copy-start.2 = (f32[4096]{0:T(1024)S(1)}, f32[4096]{0:T(1024)}, u32[]{:S(2)}) copy-start(f32[4096]{0:T(1024)} %param.11) | copy-start | bytes 49156
  7.2 158.4 %reduce-scatter.16.cloned.1.call-start = ((), (), s32[]{:S(2)}) async-start(), calls=%async_computation.5 | async-start | bytes 327680
  8.0 230.4 %collective-permute-start = (f32[4,2,8,128]{3,2,0,1:T(8,128)S(1)}, f32[4,2,8,128]{3,2,0,1:T(8,128)S(1)}, u32[]{:S(2)}, u32[]{:S(2)}) collective-permute-start(f32[4,2,8,128]{3,2,0,1:T(8,128)S(1)} %get-tuple-element.52), channel_id=1, source_target_pairs={{0,4},{4,8},{8,12},{12,16},{16,20},{20,24},{24,28},{28,0},{1,5},{5... | collective-permute-start | bytes 98312 | tf_op jit(solution)/shard_map/ppermute | solution.py:21
  8.5 229.9 %collective-permute-start.1 = (f32[4,2,8,128]{3,2,0,1:T(8,128)S(1)}, f32[4,2,8,128]{3,2,0,1:T(8,128)S(1)}, u32[]{:S(2)}, u32[]{:S(2)}) collective-permute-start(f32[4,2,8,128]{3,2,0,1:T(8,128)S(1)} %get-tuple-element.53), channel_id=1, source_target_pairs={{4,0},{8,4},{12,8},{16,12},{20,16},{24,20},{28,24},{0,28},{5,1},{9... | collective-permute-start | bytes 98312 | tf_op jit(solution)/shard_map/ppermute | solution.py:22
  49.0 2.5 copy-start.9
  49.0 2.5 copy-start.5
  49.0 2.6 copy-start.6
  49.0 2.6 copy-start.7
  49.0 68.1 %copy-start.3 = (f32[3,4,8,128]{3,2,1,0:T(8,128)S(1)}, f32[3,4,8,128]{3,2,1,0:T(8,128)}, u32[]{:S(2)}) copy-start(f32[3,4,8,128]{3,2,1,0:T(8,128)} %param.14) | copy-start | bytes 147460
  51.4 160.0 %reduce-scatter.18.cloned.1.call-start = ((), (), s32[]{:S(2)}) async-start(), calls=%async_computation.6 | async-start | bytes 327680
  125.6 40.9 %copy-start.11 = (f32[3,128]{1,0:T(4,128)S(1)}, f32[3,128]{1,0:T(4,128)}, u32[]{:S(2)}) copy-start(f32[3,128]{1,0:T(4,128)} %param.10) | copy-start | bytes 4612
  193.6 62.5 %reduce-scatter.20.cloned.1.call-start = ((), (), s32[]{:S(2)}) async-start(), calls=%async_computation.7 | async-start | bytes 327680
  238.4 62.5 %reduce-scatter.22.cloned.1.call-start = ((), (), s32[]{:S(2)}) async-start(), calls=%async_computation.8 | async-start | bytes 327680
  238.5 154.7 %collective-permute-start.2 = (f32[4,8,2,128]{3,2,0,1:T(2,128)S(1)}, f32[4,8,2,128]{3,2,0,1:T(2,128)S(1)}, u32[]{:S(2)}, u32[]{:S(2)}) collective-permute-start(f32[4,8,2,128]{3,2,0,1:T(2,128)S(1)} %get-tuple-element.45), channel_id=1, source_target_pairs={{0,1},{1,2},{2,3},{3,0},{4,5},{5,6},{6,7},{7,4},{8,9},{9,10},{10,1... | collective-permute-start | bytes 98312 | tf_op jit(solution)/shard_map/ppermute | solution.py:21
  238.5 154.6 %collective-permute-start.3 = (f32[4,8,2,128]{3,2,0,1:T(2,128)S(1)}, f32[4,8,2,128]{3,2,0,1:T(2,128)S(1)}, u32[]{:S(2)}, u32[]{:S(2)}) collective-permute-start(f32[4,8,2,128]{3,2,0,1:T(2,128)S(1)} %get-tuple-element.44), channel_id=1, source_target_pairs={{1,0},{2,1},{3,2},{0,3},{5,4},{6,5},{7,6},{4,7},{9,8},{10,9},{11,1... | collective-permute-start | bytes 98312 | tf_op jit(solution)/shard_map/ppermute | solution.py:22
  283.2 109.1 %reduce-scatter.24.cloned.1.call-start = ((), (), s32[]{:S(2)}) async-start(), calls=%async_computation.9 | async-start | bytes 327680
  301.8 26.5 %copy-start.10 = (f32[3,128]{1,0:T(4,128)}, f32[3,128]{1,0:T(4,128)S(1)}, u32[]{:S(2)}) copy-start(f32[3,128]{1,0:T(4,128)S(1)} %multiply_add_fusion.5) | copy-start | bytes 4612
  417.0 8.3 %copy-start.8 = (f32[3,4,8,128]{3,2,1,0:T(8,128)S(1)}, f32[3,4,8,128]{3,2,1,0:T(8,128)}, u32[]{:S(2)}) copy-start(f32[3,4,8,128]{3,2,1,0:T(8,128)} %param.15) | copy-start | bytes 147460
  425.3 84.9 %copy-start.4 = (f32[3,4,8,128]{3,2,1,0:T(8,128)}, f32[3,4,8,128]{3,2,1,0:T(8,128)S(1)}, u32[]{:S(2)}) copy-start(f32[3,4,8,128]{3,2,1,0:T(8,128)S(1)} %get-tuple-element.32) | copy-start | bytes 147460
  432.2 46.2 %collective-permute-start.4 = (f32[4,2,8,128]{3,2,1,0:T(8,128)S(1)}, f32[4,2,8,128]{3,2,1,0:T(8,128)S(1)}, u32[]{:S(2)}, u32[]{:S(2)}) collective-permute-start(f32[4,2,8,128]{3,2,1,0:T(8,128)S(1)} %get-tuple-element.48), channel_id=1, source_target_pairs={{0,4},{4,8},{8,12},{12,16},{16,20},{20,24},{24,28},{28,0},{1,5},{5... | collective-permute-start | bytes 98312 | tf_op jit(solution)/shard_map/ppermute | solution.py:21
  432.2 46.1 %collective-permute-start.5 = (f32[4,2,8,128]{3,2,1,0:T(8,128)S(1)}, f32[4,2,8,128]{3,2,1,0:T(8,128)S(1)}, u32[]{:S(2)}, u32[]{:S(2)}) collective-permute-start(f32[4,2,8,128]{3,2,1,0:T(8,128)S(1)} %get-tuple-element.49), channel_id=1, source_target_pairs={{4,0},{8,4},{12,8},{16,12},{20,16},{24,20},{28,24},{0,28},{5,1},{9... | collective-permute-start | bytes 98312 | tf_op jit(solution)/shard_map/ppermute | solution.py:22
  478.4 5.8 %collective-permute-start.6 = (f32[4,8,2,128]{3,2,1,0:T(2,128)S(1)}, f32[4,8,2,128]{3,2,1,0:T(2,128)S(1)}, u32[]{:S(2)}, u32[]{:S(2)}) collective-permute-start(f32[4,8,2,128]{3,2,1,0:T(2,128)S(1)} %get-tuple-element.41), channel_id=1, source_target_pairs={{0,1},{1,2},{2,3},{3,0},{4,5},{5,6},{6,7},{7,4},{8,9},{9,10},{10,1... | collective-permute-start | bytes 98312 | tf_op jit(solution)/shard_map/ppermute | solution.py:21
  478.4 5.8 %collective-permute-start.7 = (f32[4,8,2,128]{3,2,1,0:T(2,128)S(1)}, f32[4,8,2,128]{3,2,1,0:T(2,128)S(1)}, u32[]{:S(2)}, u32[]{:S(2)}) collective-permute-start(f32[4,8,2,128]{3,2,1,0:T(2,128)S(1)} %get-tuple-element.40), channel_id=1, source_target_pairs={{1,0},{2,1},{3,2},{0,3},{5,4},{6,5},{7,6},{4,7},{9,8},{10,9},{11,1... | collective-permute-start | bytes 98312 | tf_op jit(solution)/shard_map/ppermute | solution.py:22
  509.4 9.5 %copy-start.1 = (s32[4096,4]{0,1:T(4,128)S(1)}, s32[4096,4]{0,1:T(4,128)}, u32[]{:S(2)}) copy-start(s32[4096,4]{0,1:T(4,128)} %param.13) | copy-start | bytes 196612
Sparse Core Ops, SparseCore 0:
  51.5 18.8 reduce-scatter.15
  193.7 17.5 reduce-scatter.17
  238.5 17.6 reduce-scatter.19
  283.3 17.5 reduce-scatter.21
  328.4 17.6 reduce-scatter.23
where the time goes:
time: 531 us; the launch traced here: 526 us
  blocking collectives  315 us (59%)
  other arithmetic  76.8 us (14%)
  waiting for transfers between devices  50.8 us (10%)
  matrix products  34.2 us (6%)
  local copies, waits for them, and re-layouts  19.3 us (4%)
  between operations  15.2 us (3%)
  starting transfers between devices  14.4 us (3%)
    all_gather x2, blocking collectives, slow_both(): everyone = lax.all_gather(frac, ('row', 'col'), axis=1, tiled=True)  129 us
    psum x2, blocking collectives, slow_both(): summed = lax.psum(partial_env, ('row', 'col'))  78.8 us
    all_gather x5, blocking collectives, fast_force(): rows_pos = lax.all_gather(frac, 'col', axis=1, tiled=True)  60.6 us
    unnamed x10, waiting for transfers between devices  49.2 us
    all_gather x5, blocking collectives, fast_force(): cols_pos = lax.all_gather(frac, 'row', axis=1, tiled=True)  45.9 us
    reduce_sum x4, other arithmetic, slow_cells(): force = force + jnp.sum(weight[None] * delta, axis=-1)  30.7 us
    dot_general x10, matrix products, slow_cells(): jnp.einsum('abo,oxabn->xabn', pick, views, precision=lax.Precision.HIGHEST)  20.6 us
    dot_general x2, matrix products, slow_both(): jnp.dot(select, table, precision=lax.Precision.HIGHEST, preferred_element...  13.6 us
  transfers between devices with their start and end apart: 13, of which 5 were waited for; matrix products, arithmetic and copies ran while one was open for 11% of the time, Pallas kernels for 0%

commit v1 on v0

--- a/solution.py
+++ b/solution.py
@@ -131,7 +131,10 @@
             [padded[:, o // 5 : o // 5 + cell_rows, o % 5 : o % 5 + cell_cols] for o in range(25)]
         )
         cell_force = slow_cells(data, views, neighbours)
-        everyone = lax.all_gather(frac, ("row", "col"), axis=1, tiled=True)
+        everyone = jnp.concatenate(
+            lax.all_to_all(jnp.stack([frac] * lax.axis_size(("row", "col"))), ("row", "col"), 0, 0),
+            axis=1,
+        )
         table = jnp.transpose(data, (1, 2, 0, 3)).reshape(cell_rows * cell_cols, 4 * CELL)
         picked = jnp.dot(
             select, table, precision=lax.Precision.HIGHEST, preferred_element_type=jnp.float32

time: 531 us -> 434 us (0.82)
  blocking collectives: 315 us -> 185 us
  other arithmetic: 76.8 us -> 91.5 us
  starting transfers between devices: 14.4 us -> 21.2 us
    all_gather x2 -> x0, blocking collectives: 129 us -> none  [slow_both(): everyone = lax.all_gather(frac, ('row', 'col'), axis=1, tiled=True)]
    all_to_all x0 -> x2, starting transfers between devices: none -> 6.16 us  [slow_both(): lax.all_to_all(jnp.stack([frac] * lax.axis_size(('row', 'col'))), ('row',...]
    reduce_sum x2, other arithmetic: 1.69 us -> 7.73 us  [fast_from_cells(): dist_sq = jnp.sum(delta * delta, axis=0) + 0.5]
    reduce_sum x2, other arithmetic: 2.11 us -> 7.75 us  [fast_from_cells(): jnp.sum(weight[None] * delta, axis=-1)]
  transfers between devices with their start and end apart: 13 -> 15, of which waited for: 5 -> 6; matrix products, arithmetic and copies ran while one was open for 11% -> 31% of each run, Pallas kernels for 0% -> 0%
where the time goes in v1:
time: 434 us; the launch traced here: 426 us
  blocking collectives  185 us (43%)
  other arithmetic  91.5 us (21%)
  waiting for transfers between devices  53.9 us (12%)
  matrix products  38.5 us (9%)
  starting transfers between devices  21.2 us (5%)
  local copies, waits for them, and re-layouts  20.7 us (5%)
  between operations  15.5 us (4%)
    psum x2, blocking collectives, slow_both(): summed = lax.psum(partial_env, ('row', 'col'))  78.5 us
    all_gather x5, blocking collectives, fast_force(): rows_pos = lax.all_gather(frac, 'col', axis=1, tiled=True)  60.6 us
    unnamed x10, waiting for transfers between devices  52.3 us
    all_gather x5, blocking collectives, fast_force(): cols_pos = lax.all_gather(frac, 'row', axis=1, tiled=True)  46 us
    reduce_sum x4, other arithmetic, slow_cells(): force = force + jnp.sum(weight[None] * delta, axis=-1)  30.5 us
    dot_general x10, matrix products, slow_cells(): jnp.einsum('abo,oxabn->xabn', pick, views, precision=lax.Precision.HIGHEST)  20.6 us
    dot_general x2, matrix products, slow_both(): jnp.dot(select, table, precision=lax.Precision.HIGHEST, preferred_element...  17.9 us
    ppermute x4, starting transfers between devices, with_halo(): after = lax.ppermute(initial, axis, down)  14 us
  transfers between devices with their start and end apart: 15, of which 6 were waited for; matrix products, arithmetic and copies ran while one was open for 31% of the time, Pallas kernels for 0%

profile of v1, /device:TPU:0, one launch (start us, length us, event | category | flops | bytes accessed | tf_op | source)
XLA Modules:
  0.0 426.2 jit_solution(2174839411865131301)
XLA Ops:
  8.5 2.9 collective-permute-start.1
  11.6 9.6 %all_gather.31 = f32[3,1024]{1,0:T(4,128)S(1)} all-gather(f32[3,128]{1,0:T(4,128)} %param.9), channel_id=1, replica_groups=mesh['row'=8,'col'=4] {'row'}, dimensions={1}, use_global_device_ids=true | all-gather | bytes 13824 | tf_op jit(solution)/shard_map/all_gather | solution.py:103
  21.2 12.3 %all_gather.30 = f32[3,512]{1,0:T(4,128)S(1)} all-gather(f32[3,128]{1,0:T(4,128)} %param.9), channel_id=1, replica_groups=mesh['row'=8,'col'=4] {'col'}, dimensions={1}, use_global_device_ids=true | all-gather | bytes 7680 | tf_op jit(solution)/shard_map/all_gather | solution.py:102
  35.2 6.1 %gather_fusion = f32[1024]{0:T(1024)S(1)} fusion(f32[4096]{0:T(1024)S(1)} %copy-done.2, s32[1024]{0:T(1024)S(1)} %broadcast_clamp_fusion), kind=kCustom, calls=%fused_computation | custom fusion | bytes 12288 | tf_op jit(solution)/shard_map/jit(_take)/gather | solution.py:99
  52.1 3.4 all-to-all-start
  55.8 8.9 %convolution_bitcast_fusion.1 = f32[4,4096,128]{1,2,0:T(8,128)} fusion(s32[4096]{0:T(1024)S(1)} %get-tuple-element.54, pred[4096]{0:T(1024)(128)(4,1)S(1)} %compare_and_fusion, f32[1,4,8,128]{3,2,0,1:T(8,128)S(1)} %bitcast.464, f32[3,4,8,128]{3,2,1,0:T(8,128)S(1)} %copy-done.3), kind=kOutput, calls=%fused_computation.29 | convolution fusion | flops 805715968 | bytes 8474624 | tf_op jit(solution)/shard_map/dot_general | solution.py:139
  64.8 6.4 %reduce-scatter.16.cloned.1.call-done = f32[128,3]{1,0:T(8,128)} async-done(((f32[512,3]{1,0:T(8,128)}), f32[128,3]{1,0:T(8,128)}) %reduce-scatter.16.cloned.1.call-update) | async-done | bytes 1552
  72.2 4.3 %collective-permute-start.3 = (f32[4,8,2,128]{3,2,0,1:T(2,128)S(1)}, f32[4,8,2,128]{3,2,0,1:T(2,128)S(1)}, u32[]{:S(2)}, u32[]{:S(2)}) collective-permute-start(f32[4,8,2,128]{3,2,0,1:T(2,128)S(1)} %get-tuple-element.44), channel_id=1, source_target_pairs={{1,0},{2,1},{3,2},{0,3},{5,4},{6,5},{7,6},{4,7},{9,8},{10,9},{11,1... | collective-permute-start | bytes 98312 | tf_op jit(solution)/shard_map/ppermute | solution.py:22
  92.4 7.2 %fusion.3 = (f32[3,4,8,128]{3,2,1,0:T(8,128)S(1)}, f32[4,8,128,128]{3,2,1,0:T(8,128)S(1)}, f32[4,8,128,128]{3,2,1,0:T(8,128)S(1)}, f32[4,8,128,128]{3,2,1,0:T(8,128)S(1)}, f32[3,4,8,128]{3,2,1,0:T(8,128)S(1)}) fusion(f32[4,8,128,128]{3,2,1,0:T(8,128)S(1)} %fusion.51, f32[3,4,8,128]{3,2,1,0:T(8,128)S(1)} %slice_add_fusion.8, ...), kind=kLoop, calls=%fused_computation.33 | loop fusion | flops 21995520 | bytes 10878976 | tf_op jit(solution)/shard_map/reduce_sum | solution.py:56
  101.9 8.1 %fusion.5 = (f32[3,4,8,128]{3,2,1,0:T(8,128)S(1)}, f32[3,4,8,128]{3,2,1,0:T(8,128)S(1)}, f32[3,4,8,128]{3,2,1,0:T(8,128)S(1)}) fusion(f32[4,8,128,128]{3,2,1,0:T(8,128)S(1)} %fusion.53, f32[3,4,8,128]{3,2,1,0:T(8,128)S(1)} %slice_add_fusion.7, f32[3,4,8,128]{3,2,1,0:T(8,128)S(1)} %copy-done.3, f32[3,4,8,128]{3,2,1,0:T(8,128)S(1)} %slice_add_fusion.5, ...), kind=kLoop, calls=%fused_computation.35 | loop fusion | flops 14118912 | bytes 6635520 | tf_op jit(solution)/shard_map/reduce_sum | solution.py:56
  110.0 9.0 %convolution_bitcast_fusion = f32[4,4096,128]{1,2,0:T(8,128)} fusion(s32[4096]{0:T(1024)S(1)} %get-tuple-element.54, pred[4096]{0:T(1024)(128)(4,1)S(1)} %compare_and_fusion, f32[1,4,8,128]{3,2,1,0:T(8,128)S(1)} %bitcast.469, f32[3,4,8,128]{3,2,1,0:T(8,128)S(1)} %get-tuple-element.32), kind=kOutput, calls=%fused_computation.28 | convolution fusion | flops 805715968 | bytes 8474624 | tf_op jit(solution)/shard_map/dot_general | solution.py:139
  119.1 3.0 collective-permute-start.5
  122.1 3.9 multiply_reduce_fusion.13
  128.3 3.9 multiply_reduce_fusion.12
  132.2 39.7 %psum.14 = f32[3,4096]{1,0:T(4,128)S(1)} all-reduce(f32[3,4096]{1,0:T(4,128)S(1)} %broadcast_multiply_fusion.1), channel_id=1, replica_groups=mesh['row'=8,'col'=4] {'row','col'}, use_global_device_ids=true, to_apply=%region_2.3 | all-reduce | flops 12288 | bytes 98304 | tf_op jit(solution)/shard_map/psum | solution.py:144
  172.0 9.7 %all_gather.33 = f32[3,1024]{1,0:T(4,128)S(1)} all-gather(f32[3,128]{1,0:T(4,128)S(1)} %get-tuple-element.36), channel_id=1, replica_groups=mesh['row'=8,'col'=4] {'row'}, dimensions={1}, use_global_device_ids=true | all-gather | bytes 13824 | tf_op jit(solution)/shard_map/all_gather | solution.py:103
  181.6 12.5 %all_gather.32 = f32[3,512]{1,0:T(4,128)S(1)} all-gather(f32[3,128]{1,0:T(4,128)S(1)} %get-tuple-element.36), channel_id=1, replica_groups=mesh['row'=8,'col'=4] {'col'}, dimensions={1}, use_global_device_ids=true | all-gather | bytes 7680 | tf_op jit(solution)/shard_map/all_gather | solution.py:102
  199.7 3.7 collective-permute-start.7
  203.4 13.8 %reduce-scatter.18.cloned.1.call-done = f32[128,3]{1,0:T(8,128)} async-done(((f32[512,3]{1,0:T(8,128)}), f32[128,3]{1,0:T(8,128)}) %reduce-scatter.18.cloned.1.call-update) | async-done | bytes 1552
  218.1 8.9 %all_gather.35 = f32[3,1024]{1,0:T(4,128)S(1)} all-gather(f32[3,128]{1,0:T(4,128)S(1)} %multiply_add_fusion.7), channel_id=1, replica_groups=mesh['row'=8,'col'=4] {'row'}, dimensions={1}, use_global_device_ids=true | all-gather | bytes 13824 | tf_op jit(solution)/shard_map/all_gather | solution.py:103
  227.0 11.9 %all_gather.34 = f32[3,512]{1,0:T(4,128)S(1)} all-gather(f32[3,128]{1,0:T(4,128)S(1)} %multiply_add_fusion.7), channel_id=1, replica_groups=mesh['row'=8,'col'=4] {'col'}, dimensions={1}, use_global_device_ids=true | all-gather | bytes 7680 | tf_op jit(solution)/shard_map/all_gather | solution.py:102
  244.3 17.7 %reduce-scatter.20.cloned.1.call-done = f32[128,3]{1,0:T(8,128)} async-done(((f32[512,3]{1,0:T(8,128)}), f32[128,3]{1,0:T(8,128)}) %reduce-scatter.20.cloned.1.call-update) | async-done | bytes 1552
  262.9 8.9 %all_gather.37 = f32[3,1024]{1,0:T(4,128)S(1)} all-gather(f32[3,128]{1,0:T(4,128)S(1)} %get-tuple-element.34), channel_id=1, replica_groups=mesh['row'=8,'col'=4] {'row'}, dimensions={1}, use_global_device_ids=true | all-gather | bytes 13824 | tf_op jit(solution)/shard_map/all_gather | solution.py:103
  271.8 11.9 %all_gather.36 = f32[3,512]{1,0:T(4,128)S(1)} all-gather(f32[3,128]{1,0:T(4,128)S(1)} %get-tuple-element.34), channel_id=1, replica_groups=mesh['row'=8,'col'=4] {'col'}, dimensions={1}, use_global_device_ids=true | all-gather | bytes 7680 | tf_op jit(solution)/shard_map/all_gather | solution.py:102
  305.7 7.2 %fusion.13 = (f32[3,4,8,128]{3,2,1,0:T(8,128)S(1)}, f32[4,8,128,128]{3,2,1,0:T(8,128)S(1)}, f32[4,8,128,128]{3,2,1,0:T(8,128)S(1)}, f32[4,8,128,128]{3,2,1,0:T(8,128)S(1)}, f32[3,4,8,128]{3,2,1,0:T(8,128)S(1)}) fusion(f32[4,8,128,128]{3,2,1,0:T(8,128)S(1)} %fusion.64, f32[3,4,8,128]{3,2,1,0:T(8,128)S(1)} %slice_add_fusion.3, ...), kind=kLoop, calls=%fused_computation.43 | loop fusion | flops 21995520 | bytes 10878976 | tf_op jit(solution)/shard_map/reduce_sum | solution.py:56
  315.2 8.1 %fusion.15 = (f32[3,4,8,128]{3,2,1,0:T(8,128)S(1)}, f32[3,4,8,128]{3,2,1,0:T(8,128)S(1)}, f32[3,4,8,128]{3,2,1,0:T(8,128)S(1)}) fusion(f32[4,8,128,128]{3,2,1,0:T(8,128)S(1)} %fusion.66, f32[3,4,8,128]{3,2,1,0:T(8,128)S(1)} %slice_add_fusion.2, f32[3,4,8,128]{3,2,1,0:T(8,128)S(1)} %get-tuple-element.32, f32[3,4,8,128]{3,2,1,0:T(8,128)S(1)} %slice_add_fusion, ...), kind=kLoop, calls=%fused_computation.45 | loop fusion | flops 14118912 | bytes 6635520 | tf_op jit(solution)/shard_map/reduce_sum | solution.py:56
  324.3 8.9 %all_gather.39 = f32[3,1024]{1,0:T(4,128)S(1)} all-gather(f32[3,128]{1,0:T(4,128)S(1)} %multiply_add_fusion.5), channel_id=1, replica_groups=mesh['row'=8,'col'=4] {'row'}, dimensions={1}, use_global_device_ids=true | all-gather | bytes 13824 | tf_op jit(solution)/shard_map/all_gather | solution.py:103
  333.1 11.9 %all_gather.38 = f32[3,512]{1,0:T(4,128)S(1)} all-gather(f32[3,128]{1,0:T(4,128)S(1)} %multiply_add_fusion.5), channel_id=1, replica_groups=mesh['row'=8,'col'=4] {'col'}, dimensions={1}, use_global_device_ids=true | all-gather | bytes 7680 | tf_op jit(solution)/shard_map/all_gather | solution.py:102
  354.4 14.4 %reduce-scatter.24.cloned.1.call-done = f32[128,3]{1,0:T(8,128)} async-done(((f32[512,3]{1,0:T(8,128)}), f32[128,3]{1,0:T(8,128)}) %reduce-scatter.24.cloned.1.call-update) | async-done | bytes 1552
  369.7 3.9 multiply_reduce_fusion.1
  376.0 3.9 multiply_reduce_fusion
  379.9 38.7 %psum.15 = f32[3,4096]{1,0:T(4,128)S(1)} all-reduce(f32[3,4096]{1,0:T(4,128)S(1)} %broadcast_multiply_fusion), channel_id=1, replica_groups=mesh['row'=8,'col'=4] {'row','col'}, use_global_device_ids=true, to_apply=%region_31.32 | all-reduce | flops 12288 | bytes 98304 | tf_op jit(solution)/shard_map/psum | solution.py:144
  (224 shorter events, 86.2 us)
Async XLA Ops:
  7.2 37.4 %copy-start = (s32[4096,4]{0,1:T(4,128)S(1)}, s32[4096,4]{0,1:T(4,128)}, u32[]{:S(2)}) copy-start(s32[4096,4]{0,1:T(4,128)} %param.13) | copy-start | bytes 196612
  7.2 27.9 %copy-start.2 = (f32[4096]{0:T(1024)S(1)}, f32[4096]{0:T(1024)}, u32[]{:S(2)}) copy-start(f32[4096]{0:T(1024)} %param.11) | copy-start | bytes 49156
  7.2 64.0 %reduce-scatter.16.cloned.1.call-start = ((), (), s32[]{:S(2)}) async-start(), calls=%async_computation.7 | async-start | bytes 327680
  8.0 64.0 %collective-permute-start = (f32[4,2,8,128]{3,2,0,1:T(8,128)S(1)}, f32[4,2,8,128]{3,2,0,1:T(8,128)S(1)}, u32[]{:S(2)}, u32[]{:S(2)}) collective-permute-start(f32[4,2,8,128]{3,2,0,1:T(8,128)S(1)} %get-tuple-element.52), channel_id=1, source_target_pairs={{0,4},{4,8},{8,12},{12,16},{16,20},{20,24},{24,28},{28,0},{1,5},{5... | collective-permute-start | bytes 98312 | tf_op jit(solution)/shard_map/ppermute | solution.py:21
  8.5 63.5 %collective-permute-start.1 = (f32[4,2,8,128]{3,2,0,1:T(8,128)S(1)}, f32[4,2,8,128]{3,2,0,1:T(8,128)S(1)}, u32[]{:S(2)}, u32[]{:S(2)}) collective-permute-start(f32[4,2,8,128]{3,2,0,1:T(8,128)S(1)} %get-tuple-element.53), channel_id=1, source_target_pairs={{4,0},{8,4},{12,8},{16,12},{20,16},{24,20},{28,24},{0,28},{5,1},{9... | collective-permute-start | bytes 98312 | tf_op jit(solution)/shard_map/ppermute | solution.py:22
  49.0 2.4 copy-start.7
  49.0 6.5 %copy-start.9 = (s32[4,8,5]{1,0,2:T(4,128)S(1)}, s32[4,8,5]{1,0,2:T(4,128)}, u32[]{:S(2)}) copy-start(s32[4,8,5]{1,0,2:T(4,128)} %param.17) | copy-start | bytes 1924
  49.0 6.5 %copy-start.5 = (f32[4,8,128]{2,1,0:T(8,128)S(1)}, f32[4,8,128]{2,1,0:T(8,128)}, u32[]{:S(2)}) copy-start(f32[4,8,128]{2,1,0:T(8,128)} %param.16) | copy-start | bytes 49156
  49.0 6.5 %copy-start.6 = (s32[4096]{0:T(1024)S(1)}, s32[4096]{0:T(1024)}, u32[]{:S(2)}) copy-start(s32[4096]{0:T(1024)} %param.12) | copy-start | bytes 49156
  49.0 6.7 %copy-start.3 = (f32[3,4,8,128]{3,2,1,0:T(8,128)S(1)}, f32[3,4,8,128]{3,2,1,0:T(8,128)}, u32[]{:S(2)}) copy-start(f32[3,4,8,128]{3,2,1,0:T(8,128)} %param.14) | copy-start | bytes 147460
  52.1 70.0 %all-to-all-start = ((f32[32,3,128]{2,1,0:T(4,128)}), f32[32,3,128]{2,1,0:T(4,128)S(1)}, u32[]{:S(2)}, u32[]{:S(2)}) async-start(f32[32,3,128]{2,1,0:T(4,128)} %stack.124), calls=%async_computation | async-start | bytes 131072 | tf_op jit(solution)/shard_map/all_to_all | solution.py:135
  55.4 161.8 %reduce-scatter.18.cloned.1.call-start = ((), (), s32[]{:S(2)}) async-start(), calls=%async_computation.8 | async-start | bytes 327680
  72.1 5.8 %collective-permute-start.2 = (f32[4,8,2,128]{3,2,0,1:T(2,128)S(1)}, f32[4,8,2,128]{3,2,0,1:T(2,128)S(1)}, u32[]{:S(2)}, u32[]{:S(2)}) collective-permute-start(f32[4,8,2,128]{3,2,0,1:T(2,128)S(1)} %get-tuple-element.45), channel_id=1, source_target_pairs={{0,1},{1,2},{2,3},{3,0},{4,5},{5,6},{6,7},{7,4},{8,9},{9,10},{10,1... | collective-permute-start | bytes 98312 | tf_op jit(solution)/shard_map/ppermute | solution.py:21
  72.2 5.9 %collective-permute-start.3 = (f32[4,8,2,128]{3,2,0,1:T(2,128)S(1)}, f32[4,8,2,128]{3,2,0,1:T(2,128)S(1)}, u32[]{:S(2)}, u32[]{:S(2)}) collective-permute-start(f32[4,8,2,128]{3,2,0,1:T(2,128)S(1)} %get-tuple-element.44), channel_id=1, source_target_pairs={{1,0},{2,1},{3,2},{0,3},{5,4},{6,5},{7,6},{4,7},{9,8},{10,9},{11,1... | collective-permute-start | bytes 98312 | tf_op jit(solution)/shard_map/ppermute | solution.py:22
  101.9 8.1 %copy-start.8 = (f32[3,4,8,128]{3,2,1,0:T(8,128)S(1)}, f32[3,4,8,128]{3,2,1,0:T(8,128)}, u32[]{:S(2)}) copy-start(f32[3,4,8,128]{3,2,1,0:T(8,128)} %param.15) | copy-start | bytes 147460
  110.0 205.2 %copy-start.4 = (f32[3,4,8,128]{3,2,1,0:T(8,128)}, f32[3,4,8,128]{3,2,1,0:T(8,128)S(1)}, u32[]{:S(2)}) copy-start(f32[3,4,8,128]{3,2,1,0:T(8,128)S(1)} %get-tuple-element.32) | copy-start | bytes 147460
  119.0 80.4 %collective-permute-start.4 = (f32[4,2,8,128]{3,2,1,0:T(8,128)S(1)}, f32[4,2,8,128]{3,2,1,0:T(8,128)S(1)}, u32[]{:S(2)}, u32[]{:S(2)}) collective-permute-start(f32[4,2,8,128]{3,2,1,0:T(8,128)S(1)} %get-tuple-element.48), channel_id=1, source_target_pairs={{0,4},{4,8},{8,12},{12,16},{16,20},{20,24},{24,28},{28,0},{1,5},{5... | collective-permute-start | bytes 98312 | tf_op jit(solution)/shard_map/ppermute | solution.py:21
  119.1 80.4 %collective-permute-start.5 = (f32[4,2,8,128]{3,2,1,0:T(8,128)S(1)}, f32[4,2,8,128]{3,2,1,0:T(8,128)S(1)}, u32[]{:S(2)}, u32[]{:S(2)}) collective-permute-start(f32[4,2,8,128]{3,2,1,0:T(8,128)S(1)} %get-tuple-element.49), channel_id=1, source_target_pairs={{4,0},{8,4},{12,8},{16,12},{20,16},{24,20},{28,24},{0,28},{5,1},{9... | collective-permute-start | bytes 98312 | tf_op jit(solution)/shard_map/ppermute | solution.py:22
  128.3 43.6 %copy-start.11 = (f32[3,128]{1,0:T(4,128)S(1)}, f32[3,128]{1,0:T(4,128)}, u32[]{:S(2)}) copy-start(f32[3,128]{1,0:T(4,128)} %param.10) | copy-start | bytes 4612
  199.4 62.5 %reduce-scatter.20.cloned.1.call-start = ((), (), s32[]{:S(2)}) async-start(), calls=%async_computation.9 | async-start | bytes 327680
  199.5 89.7 %collective-permute-start.6 = (f32[4,8,2,128]{3,2,1,0:T(2,128)S(1)}, f32[4,8,2,128]{3,2,1,0:T(2,128)S(1)}, u32[]{:S(2)}, u32[]{:S(2)}) collective-permute-start(f32[4,8,2,128]{3,2,1,0:T(2,128)S(1)} %get-tuple-element.41), channel_id=1, source_target_pairs={{0,1},{1,2},{2,3},{3,0},{4,5},{5,6},{6,7},{7,4},{8,9},{9,10},{10,1... | collective-permute-start | bytes 98312 | tf_op jit(solution)/shard_map/ppermute | solution.py:21
  199.7 89.5 %collective-permute-start.7 = (f32[4,8,2,128]{3,2,1,0:T(2,128)S(1)}, f32[4,8,2,128]{3,2,1,0:T(2,128)S(1)}, u32[]{:S(2)}, u32[]{:S(2)}) collective-permute-start(f32[4,8,2,128]{3,2,1,0:T(2,128)S(1)} %get-tuple-element.40), channel_id=1, source_target_pairs={{1,0},{2,1},{3,2},{0,3},{5,4},{6,5},{7,6},{4,7},{9,8},{10,9},{11,1... | collective-permute-start | bytes 98312 | tf_op jit(solution)/shard_map/ppermute | solution.py:22
  244.2 79.1 %reduce-scatter.22.cloned.1.call-start = ((), (), s32[]{:S(2)}) async-start(), calls=%async_computation.10 | async-start | bytes 327680
  289.0 79.8 %reduce-scatter.24.cloned.1.call-start = ((), (), s32[]{:S(2)}) async-start(), calls=%async_computation.11 | async-start | bytes 327680
  324.2 26.1 %copy-start.10 = (f32[3,128]{1,0:T(4,128)}, f32[3,128]{1,0:T(4,128)S(1)}, u32[]{:S(2)}) copy-start(f32[3,128]{1,0:T(4,128)S(1)} %multiply_add_fusion.5) | copy-start | bytes 4612
  351.0 18.8 %all-to-all-start.1 = ((f32[32,3,128]{2,1,0:T(4,128)}), f32[32,3,128]{2,1,0:T(4,128)S(1)}, u32[]{:S(2)}, u32[]{:S(2)}) async-start(f32[32,3,128]{2,1,0:T(4,128)} %stack.310), calls=%async_computation.1 | async-start | bytes 131072 | tf_op jit(solution)/shard_map/all_to_all | solution.py:135
  376.0 43.3 %copy-start.1 = (s32[4096,4]{0,1:T(4,128)S(1)}, s32[4096,4]{0,1:T(4,128)}, u32[]{:S(2)}) copy-start(s32[4096,4]{0,1:T(4,128)} %param.13) | copy-start | bytes 196612
Sparse Core Ops, SparseCore 0:
  51.5 19.5 reduce-scatter.15
  199.5 17.5 reduce-scatter.17
  244.3 17.5 reduce-scatter.19
  289.1 17.5 reduce-scatter.21
  350.5 18.3 reduce-scatter.23
